TPU v7x, 128 devices: a whole 4x4x4 slice. The times are simulated.
128 devices in a mesh: seq: 16 (over z_lo, x, core), db: 8 (over y, z_hi).
Axes of the slice: x: 4, y: 4, z: 4 (z_hi: 2, z_lo: 2; z = z_hi * 2 + z_lo), core: 2. Of those that a mesh axis runs over, the one named last changes fastest.
Arguments:
- hidden_in: bfloat16 [4096, 4096], P('seq'), may hold values from -4 to 4
- query_rows: bfloat16 [4096, 4096], P('seq', 'db'), may hold values from -32 to 32
- key_rows: bfloat16 [4096, 4096], P('seq', 'db'), may hold values from -32 to 32
- value_rows: bfloat16 [4096, 4096], P('seq', 'db'), may hold values from -6 to 6
- w_self_out: bfloat16 [4096, 4096], P('db'), may hold values from -0.1796875 to 0.1796875
- norm_gain: bfloat16 [4096], replicated, may hold values from 0.099609375 to 1.8984375
- w_cross_q: bfloat16 [4096, 4096], P(None, 'db'), may hold values from -2 to 2
- w_cross_k: bfloat16 [1024, 4096], P(None, 'db'), may hold values from -1 to 1
- w_cross_v: bfloat16 [1024, 4096], P(None, 'db'), may hold values from -0.1875 to 0.1875
- w_cross_out: bfloat16 [4096, 4096], P('db'), may hold values from -0.09375 to 0.09375
- enc_table: bfloat16 [64, 128, 1024], P('db'), may hold values from -6 to 6
- nb_shard: int32 [64, 2], P('seq'), may hold values from 0 to 7, all different within a row; in each aligned block of 4 rows (0 to 3, 4 to 7, ...) at most 2 rows name the same one
- nb_row: int32 [64, 2], P('seq'), may hold values from 0 to 7
Outputs:
- block_out: float32 [4096, 4096], P(('seq', 'db'))
Inputs may be any that keep to these rules, and one draw needn't show every extreme that they name: `nb_shard`: the spans held by one index of seq name each shard at most 2 times, and in the spans of some indices one shard exactly 2 times; the 2 neighbours of a span lie in different shards.
All inputs are finite; a program needn't handle non-finite values.
Results may differ from a plain program's by a relative error of at most 0.038.
Values may be sent and summed in bfloat16 or wider, within the bound.
A program may use at most 128 MiB of HBM per device.

v0:
```python
import math
import jax
import jax.numpy as jnp
from jax import lax
from jax.sharding import PartitionSpec as P

HD = 128
SPAN = 64
NEIGH = 2
NLEN = 128
NEG_BIG = -1e30


def from_behind(block, axis, distance):
    devices = range(lax.axis_size(axis))
    route = [(i - distance, i) for i in devices if i - distance in devices]
    return lax.ppermute(block, axis, route)


def attend_block(state, query_three, key_block, value_block, query_pos, key_pos, score_scale):
    run_max, run_sum, run_acc = state
    scores = (
        jnp.einsum("qhd,khd->hqk", query_three, key_block, preferred_element_type=jnp.float32)
        * score_scale
    )
    allowed = (key_pos[None, :] <= query_pos[:, None]) & (key_pos[None, :] >= 0)
    scores = jnp.where(allowed[None], scores, NEG_BIG)
    new_max = jnp.maximum(run_max, jnp.max(scores, axis=-1))
    rescale = jnp.exp(run_max - new_max)
    weights = jnp.exp(scores - new_max[..., None])
    new_sum = run_sum * rescale + jnp.sum(weights, axis=-1)
    added = jnp.einsum(
        "hqk,khd->hqd",
        weights.astype(jnp.bfloat16),
        value_block,
        preferred_element_type=jnp.float32,
    )
    return (new_max, new_sum, run_acc * rescale[..., None] + added)


def fold_piece(carried, query_three, pieces, query_pos, score_scale):
    key_piece, value_piece = pieces
    count_rows = key_piece.shape[0]
    heads_local = query_three.shape[1]
    block_rows = math.gcd(count_rows, 512)
    block_count = count_rows // block_rows
    last_query = query_pos[query_pos.shape[0] - 1]

    def one_block(block_index, state):
        key_first = block_index * block_rows

        def compute(inner):
            key_block = lax.dynamic_slice_in_dim(
                key_piece, block_index * block_rows, block_rows, 0
            ).reshape(block_rows, heads_local, HD)
            value_block = lax.dynamic_slice_in_dim(
                value_piece, block_index * block_rows, block_rows, 0
            ).reshape(block_rows, heads_local, HD)
            key_pos = key_first + jnp.arange(block_rows, dtype=jnp.int32)
            return attend_block(
                inner, query_three, key_block, value_block, query_pos, key_pos, score_scale
            )

        def unchanged(inner):
            return inner

        live = (key_first <= last_query) & (key_first + block_rows > 0)
        return lax.cond(live, compute, unchanged, state)

    return lax.fori_loop(0, block_count, one_block, carried)


def empty_state(heads_local, rows):
    return (
        jnp.full((heads_local, rows), NEG_BIG, jnp.float32),
        jnp.zeros((heads_local, rows), jnp.float32),
        jnp.zeros((heads_local, rows, HD), jnp.float32),
    )


def finish_state(state, rows, width_local):
    run_max, run_sum, run_acc = state
    return (
        (run_acc / run_sum[..., None])
        .transpose(1, 0, 2)
        .reshape(rows, width_local)
        .astype(jnp.bfloat16)
    )


def per_device(
    hidden_in,
    query_rows,
    key_rows,
    value_rows,
    w_self_out,
    norm_gain,
    w_cross_q,
    w_cross_k,
    w_cross_v,
    w_cross_out,
    enc_table,
    nb_shard,
    nb_row,
):
    tok_rows = hidden_in.shape[0]
    width_local = query_rows.shape[1]
    heads_local = width_local // HD
    db_count = lax.axis_size("db")
    seq_index = lax.axis_index("seq")
    db_index = lax.axis_index("db")
    score_scale = 1.0 / math.sqrt(HD)
    query_three = query_rows.reshape(tok_rows, heads_local, HD)
    query_pos = seq_index * tok_rows + jnp.arange(tok_rows, dtype=jnp.int32)
    initial = empty_state(heads_local, tok_rows)
    state = fold_piece(
        initial,
        query_three,
        (
            lax.all_gather(key_rows, "seq", axis=0, tiled=True),
            lax.all_gather(value_rows, "seq", axis=0, tiled=True),
        ),
        query_pos,
        score_scale,
    )
    attended = finish_state(state, tok_rows, width_local)
    share_rows = tok_rows // db_count
    attn_total = lax.psum(
        jnp.dot(attended, w_self_out, preferred_element_type=jnp.float32).astype(jnp.bfloat16), "db"
    ).astype(jnp.float32)
    residual = hidden_in.astype(jnp.float32) + attn_total
    mean_square = jnp.mean(residual * residual, axis=-1, keepdims=True)
    normed = (residual * lax.rsqrt(mean_square + 1e-05) * norm_gain.astype(jnp.float32)).astype(
        jnp.bfloat16
    )
    cross_query = jnp.dot(normed, w_cross_q, preferred_element_type=jnp.float32).astype(
        jnp.bfloat16
    )
    span_count = tok_rows // SPAN
    entry_count = span_count * NEIGH
    capacity = 2 * ((entry_count + db_count - 1) // db_count)
    shard_flat = nb_shard.reshape(entry_count)
    row_flat = nb_row.reshape(entry_count)
    entry_ids = jnp.arange(entry_count, dtype=jnp.int32)
    earlier = (shard_flat[:, None] == shard_flat[None, :]) & (
        entry_ids[None, :] < entry_ids[:, None]
    )
    rank_flat = jnp.sum(earlier.astype(jnp.int32), axis=1)
    slot_ids = jnp.arange(capacity, dtype=jnp.int32)
    chosen = ((shard_flat[None, :] == db_index) & (rank_flat[None, :] == slot_ids[:, None])).astype(
        jnp.int32
    )
    pick_rows = jnp.sum(chosen * row_flat[None, :], axis=1)
    live_slot = jnp.sum(chosen, axis=1) > 0
    picked = jnp.take(enc_table, pick_rows, axis=0)
    outgoing = jnp.where(live_slot[:, None, None], picked, jnp.zeros_like(picked))
    arrived = lax.all_gather(outgoing, "db", axis=0, tiled=True)
    wanted = jnp.take(arrived, shard_flat * capacity + rank_flat, axis=0).reshape(
        entry_count * NLEN, enc_table.shape[2]
    )
    cross_keys = jnp.dot(wanted, w_cross_k, preferred_element_type=jnp.float32).astype(jnp.bfloat16)
    cross_values = jnp.dot(wanted, w_cross_v, preferred_element_type=jnp.float32).astype(
        jnp.bfloat16
    )
    cross_pair = jnp.stack((cross_keys, cross_values)).reshape(
        2, span_count, NEIGH * NLEN, width_local
    )
    previous = from_behind(cross_pair[:, span_count - 1], "seq", 1)
    extended = jnp.concatenate((previous[:, None], cross_pair), axis=1).reshape(
        2, span_count + 1, NEIGH * NLEN, heads_local, HD
    )
    padded = jnp.pad(cross_query, ((1, SPAN - 1), (0, 0))).reshape(
        span_count + 1, SPAN, heads_local, HD
    )
    scores = (
        jnp.einsum("gqhd,gkhd->ghqk", padded, extended[0], preferred_element_type=jnp.float32)
        * score_scale
    )
    top_score = jnp.max(scores, axis=-1, keepdims=True)
    weights = jnp.exp(scores - top_score)
    totals = jnp.sum(weights, axis=-1, keepdims=True)
    mixed = (
        jnp.einsum(
            "ghqk,gkhd->ghqd",
            weights.astype(jnp.bfloat16),
            extended[1],
            preferred_element_type=jnp.float32,
        )
        / totals
    )
    cross_mixed = (
        mixed.transpose(0, 2, 1, 3)
        .reshape((span_count + 1) * SPAN, width_local)[1 : tok_rows + 1]
        .astype(jnp.bfloat16)
    )
    cross_share = lax.psum_scatter(
        jnp.dot(cross_mixed, w_cross_out, preferred_element_type=jnp.float32).astype(jnp.bfloat16),
        "db",
        scatter_dimension=0,
        tiled=True,
    ).astype(jnp.float32)
    own_residual = lax.dynamic_slice_in_dim(residual, db_index * share_rows, share_rows, 0)
    return own_residual + cross_share


def solution(mesh):
    placed = (
        P("seq", None),
        P("seq", "db"),
        P("seq", "db"),
        P("seq", "db"),
        P("db", None),
        P(),
        P(None, "db"),
        P(None, "db"),
        P(None, "db"),
        P("db", None),
        P("db", None, None),
        P("seq", None),
        P("seq", None),
    )
    return jax.shard_map(
        per_device, mesh=mesh, in_specs=placed, out_specs=P(("seq", "db"), None), check_vma=False
    )
```

profile of v0, /device:TPU:0, one launch (start us, length us, event | category | flops | bytes accessed | tf_op | source)
XLA Modules:
  0.0 419.2 jit_solution(12266112979966981673)
XLA Ops:
  6.6 0.9 copy.65
  7.6 0.8 copy.64
  8.4 0.2 convert_reduce_fusion
  8.6 0.1 convert_reduce_fusion.1
  8.8 0.6 gather_fusion
  9.4 0.9 select_select_fusion
  10.4 0.8 copy.59
  11.3 0.8 copy.61
  12.3 0.1 copy.66
  12.4 0.1 mul.98
  12.5 0.7 slice.18
  13.1 0.1 copy.60
  13.3 0.2 copy.62
  13.5 71.1 %all-gather.8.cloned.1.call-done = bf16[16,128,1024]{2,1,0:T(8,128)(2,1)} async-done(((bf16[2,128,1024]{2,1,0:T(8,128)(2,1)}), bf16[16,128,1024]{2,1,0:T(8,128)(2,1)}) %all-gather.8.cloned.1.call-update) | async-done | bytes 4194320 | tf_op jit(solution)/shard_map/all_gather | solution.py:157
  84.6 2.9 gather_fusion.1
  87.5 41.5 %all-gather.4.cloned.1.call-done = bf16[4096,512]{0,1:T(8,128)(2,1)} async-done(((bf16[256,512]{0,1:T(8,128)(2,1)}), bf16[4096,512]{0,1:T(8,128)(2,1)}) %all-gather.4.cloned.1.call-update) | async-done | bytes 4194320 | tf_op jit(solution)/shard_map/all_gather | solution.py:120
  129.0 46.8 %all-gather.6.cloned.1.call-done = bf16[4096,512]{0,1:T(8,128)(2,1)} async-done(((bf16[256,512]{0,1:T(8,128)(2,1)}), bf16[4096,512]{0,1:T(8,128)(2,1)}) %all-gather.6.cloned.1.call-update) | async-done | bytes 4194320 | tf_op jit(solution)/shard_map/all_gather | solution.py:121
  175.8 8.5 %while.18 = (s32[]{:T(128)}, f32[4,256]{1,0:T(4,128)S(1)}, f32[4,256]{1,0:T(4,128)S(1)}, f32[4,256,128]{2,1,0:T(8,128)S(1)}, s32[]{:T(128)}, /*index=5*/bf16[409...) while((s32[]{:T(128)}, f32[4,256]{1,0:T(4,128)S(1)}, ...), condition=%wide.region_5.6_spmd.clone, body=%wide.region_0.5_spmd.clone.sunk | while | flops 272633600 | bytes 11085173 | solution.py:70
  176.4 3.1 conditional.3
  176.5 0.2 compare_and_fusion
  176.7 1.3 constant_dynamic-slice_fusion
  178.0 0.6 fusion.22
  178.6 0.3 fusion.3
  178.9 0.6 convolution_add_fusion
  184.3 0.2 copy.63
  184.6 4.8 %convolution_convert_fusion.1 = bf16[256,4096]{1,0:T(8,128)(2,1)} fusion(bf16[256,512]{0,1:T(8,128)(2,1)S(1)} %bitcast.62, bf16[512,4096]{1,0:T(8,128)(2,1)} %param.21), kind=kOutput, calls=%fused_computation.18 | convolution fusion | flops 1074790400 | bytes 6553600 | tf_op jit(solution)/shard_map/dot_general | solution.py:129
  189.5 0.4 bitcast_select_fusion.1
  189.9 0.8 copy-done.12
  190.7 1.2 convolution_convert_fusion.3
  192.0 0.5 copy.67
  192.5 3.1 convolution_convert_fusion.2
  195.6 0.5 copy.68
  196.2 2.4 collective-permute-start
  198.6 1.3 collective-permute-done
  199.9 0.3 maximum_maximum_fusion
  200.2 0.2 fusion.23
  200.4 121.6 %all-reduce.3.cloned.1.call-done = bf16[256,4096]{1,0:T(8,128)(2,1)} async-done(((bf16[256,4096]{1,0:T(8,128)(2,1)}), bf16[256,4096]{1,0:T(8,128)(2,1)}) %all-reduce.3.cloned.1.call-update) | async-done | bytes 2097168 | tf_op jit(solution)/shard_map/psum | solution.py:128
  322.0 5.2 %convert_add_fusion = (f32[256,4096]{1,0:T(8,128)}, f32[256]{0:T(256)S(1)}) fusion(bf16[256,4096]{1,0:T(8,128)(2,1)} %all-reduce.3.cloned.1.call-done, bf16[256,4096]{1,0:T(8,128)(2,1)} %param.17), kind=kLoop, calls=%fused_computation.21 | loop fusion | flops 5242624 | bytes 8389632 | tf_op jit(solution)/shard_map/add | solution.py:131
  327.2 1.0 copy-done.10
  328.2 1.3 fusion.11
  329.7 0.4 fusion.24
  330.1 0.5 fusion.12
  330.6 0.7 fusion.10
  331.2 0.3 copy.73
  331.6 1.2 copy-done.11
  332.8 2.6 convolution_convert_fusion
  335.4 75.3 %reduce-scatter.2.cloned.1.call-done = bf16[32,4096]{1,0:T(8,128)(2,1)} async-done(((bf16[256,4096]{1,0:T(8,128)(2,1)}), bf16[32,4096]{1,0:T(8,128)(2,1)}) %reduce-scatter.2.cloned.1.call-update) | async-done | bytes 262160 | tf_op jit(solution)/shard_map/reduce_scatter | solution.py:196
  410.7 2.0 convert_add_fusion.1
  (75 shorter events, 1.2 us)
Async XLA Ops:
  6.5 2.3 copy-start
  6.5 3.9 copy-start.5
  6.5 4.8 %copy-start.6 = (bf16[256,512]{1,0:T(8,128)(2,1)S(1)}, bf16[256,512]{1,0:T(8,128)(2,1)}, u32[]{:S(2)}) copy-start(bf16[256,512]{1,0:T(8,128)(2,1)} %param.20) | copy-start | bytes 786436
  6.5 78.1 %all-gather.8.cloned.1.call-start = ((), (), s32[]{:S(2)}) async-start(), calls=%async_computation.4 | async-start | bytes 4718592 | tf_op jit(solution)/shard_map/all_gather | solution.py:157
  8.8 3.5 copy-start.9
  8.8 4.3 %copy-start.7 = (bf16[256,512]{1,0:T(8,128)(2,1)S(1)}, bf16[256,512]{1,0:T(8,128)(2,1)}, u32[]{:S(2)}) copy-start(bf16[256,512]{1,0:T(8,128)(2,1)} %param.18) | copy-start | bytes 786436
  10.4 118.6 %all-gather.4.cloned.1.call-start = ((), (), s32[]{:S(2)}) async-start(), calls=%async_computation.1 | async-start | bytes 4456448 | tf_op jit(solution)/shard_map/all_gather | solution.py:120
  11.3 164.5 %all-gather.6.cloned.1.call-start = ((), (), s32[]{:S(2)}) async-start(), calls=%async_computation.2 | async-start | bytes 4456448 | tf_op jit(solution)/shard_map/all_gather | solution.py:121
  12.2 309.8 %all-reduce.3.cloned.1.call-start = ((), (), s32[]{:S(2)}) async-start(), calls=%async_computation.3 | async-start | bytes 4194304 | tf_op jit(solution)/shard_map/psum | solution.py:128
  189.4 1.2 copy-start.12
  189.4 221.3 %reduce-scatter.2.cloned.1.call-start = ((), (), s32[]{:S(2)}) async-start(), calls=%async_computation.5 | async-start | bytes 2359296 | tf_op jit(solution)/shard_map/reduce_scatter | solution.py:196
  190.7 1.3 copy-start.4
  195.6 3.0 copy-start.8
  196.2 3.7 collective-permute-start
  322.0 5.2 %copy-start.2 = (bf16[256,4096]{1,0:T(8,128)(2,1)S(1)}, bf16[256,4096]{1,0:T(8,128)(2,1)}, u32[]{:S(2)}) copy-start(bf16[256,4096]{1,0:T(8,128)(2,1)} %param.17) | copy-start | bytes 6291460
  322.0 5.2 %copy-start.3 = (bf16[256,4096]{1,0:T(8,128)(2,1)S(1)}, bf16[256,4096]{1,0:T(8,128)(2,1)}, u32[]{:S(2)}) copy-start(bf16[256,4096]{1,0:T(8,128)(2,1)} %all-reduce.3.cloned.1.call-done) | copy-start | bytes 6291460
  322.0 6.2 %copy-start.10 = (bf16[4096,512]{1,0:T(8,128)(2,1)S(1)}, bf16[4096,512]{1,0:T(8,128)(2,1)}, u32[]{:S(2)}) copy-start(bf16[4096,512]{1,0:T(8,128)(2,1)} %param.23) | copy-start | bytes 12582916
  330.6 2.2 copy-start.11
  332.8 79.9 %copy-start.1 = (bf16[8,128,1024]{2,1,0:T(8,128)(2,1)S(1)}, bf16[8,128,1024]{2,1,0:T(8,128)(2,1)}, u32[]{:S(2)}) copy-start(bf16[8,128,1024]{2,1,0:T(8,128)(2,1)} %param.27) | copy-start | bytes 6291460
Sparse Core Ops, SparseCore 0:
  10.5 74.0 all-gather.7
  86.2 42.6 all-gather.3
  130.6 45.1 all-gather.5
  189.5 132.3 all-reduce.2
  335.5 75.1 reduce-scatter.1
where the time goes:
time: 420 us; the launch traced here: 419 us
  waiting for transfers between devices  358 us (85%)
  matrix products  15.3 us (4%)
  local copies, waits for them, and re-layouts  14.5 us (3%)
  between operations  13.5 us (3%)
  other arithmetic  10.3 us (2%)
  loops' own time  5.49 us (1%)
    psum x1, waiting for transfers between devices, per_device(): lax.psum(jnp.dot(attended, w_self_out, preferred_element_type=jnp.float32...  122 us
    reduce_scatter x1, waiting for transfers between devices, per_device(): lax.psum_scatter(jnp.dot(cross_mixed, w_cross_out, preferred_element_type...  75.3 us
    all_gather x1, waiting for transfers between devices, per_device(): arrived = lax.all_gather(outgoing, 'db', axis=0, tiled=True)  71.1 us
    all_gather x1, waiting for transfers between devices, per_device(): lax.all_gather(value_rows, 'seq', axis=0, tiled=True)  46.8 us
    all_gather x1, waiting for transfers between devices, per_device(): lax.all_gather(key_rows, 'seq', axis=0, tiled=True)  41.5 us
  transfers between devices with their start and end apart: 6, of which 6 were waited for; matrix products, arithmetic and copies ran while one was open for 3% of the time, Pallas kernels for 0%

commit v1 on v0

--- a/solution.py
+++ b/solution.py
@@ -9,6 +9,10 @@
 NEIGH = 2
 NLEN = 128
 NEG_BIG = -1e30
+
+
+def read_hubs(vec):
+    return lax.all_gather(vec, axis_name="db").sum(axis=0)
 
 
 def from_behind(block, axis, distance):
@@ -125,8 +129,8 @@
     )
     attended = finish_state(state, tok_rows, width_local)
     share_rows = tok_rows // db_count
-    attn_total = lax.psum(
-        jnp.dot(attended, w_self_out, preferred_element_type=jnp.float32).astype(jnp.bfloat16), "db"
+    attn_total = read_hubs(
+        jnp.dot(attended, w_self_out, preferred_element_type=jnp.float32).astype(jnp.bfloat16)
     ).astype(jnp.float32)
     residual = hidden_in.astype(jnp.float32) + attn_total
     mean_square = jnp.mean(residual * residual, axis=-1, keepdims=True)

time: 420 us -> 470 us (1.12)
  waiting for transfers between devices: 358 us -> 396 us
  other arithmetic: 10.3 us -> 18.6 us
    all_gather x0 -> x1, waiting for transfers between devices: none -> 174 us  [read_hubs(): return lax.all_gather(vec, axis_name='db').sum(axis=0)]
    psum x1 -> x0, waiting for transfers between devices: 122 us -> none  [per_device(): lax.psum(jnp.dot(attended, w_self_out, preferred_element_type=jnp.float32...]
    all_gather x1, waiting for transfers between devices: 71.1 us -> 59.1 us  [per_device(): arrived = lax.all_gather(outgoing, 'db', axis=0, tiled=True)]
    reduce_sum x0 -> x1, other arithmetic: none -> 9.16 us  [read_hubs(): return lax.all_gather(vec, axis_name='db').sum(axis=0)]
  transfers between devices with their start and end apart: 6 -> 6, of which waited for: 6 -> 6; matrix products, arithmetic and copies ran while one was open for 3% -> 5% of each run, Pallas kernels for 0% -> 0%
where the time goes in v1:
time: 470 us; the launch traced here: 469 us
  waiting for transfers between devices  396 us (84%)
  other arithmetic  18.6 us (4%)
  local copies, waits for them, and re-layouts  17.6 us (4%)
  matrix products  15.4 us (3%)
  between operations  13.4 us (3%)
  loops' own time  5.89 us (1%)
    all_gather x1, waiting for transfers between devices, read_hubs(): return lax.all_gather(vec, axis_name='db').sum(axis=0)  174 us
    reduce_scatter x1, waiting for transfers between devices, per_device(): lax.psum_scatter(jnp.dot(cross_mixed, w_cross_out, preferred_element_type...  73.4 us
    all_gather x1, waiting for transfers between devices, per_device(): arrived = lax.all_gather(outgoing, 'db', axis=0, tiled=True)  59.1 us
    all_gather x1, waiting for transfers between devices, per_device(): lax.all_gather(value_rows, 'seq', axis=0, tiled=True)  46.8 us
    all_gather x1, waiting for transfers between devices, per_device(): lax.all_gather(key_rows, 'seq', axis=0, tiled=True)  41.3 us
  transfers between devices with their start and end apart: 6, of which 6 were waited for; matrix products, arithmetic and copies ran while one was open for 5% of the time, Pallas kernels for 0%

profile of v1, /device:TPU:0, one launch (start us, length us, event | category | flops | bytes accessed | tf_op | source)
XLA Modules:
  0.0 469.1 jit_solution(8208925755443001170)
XLA Ops:
  6.5 2.0 copy.59
  8.6 1.8 copy.61
  10.5 0.8 copy.64
  11.3 0.8 copy.65
  12.2 0.2 convert_reduce_fusion
  12.4 0.2 convert_reduce_fusion.1
  12.6 0.6 gather_fusion
  13.2 0.9 select_select_fusion
  14.2 0.6 slice.18
  14.8 0.1 copy.60
  15.0 0.2 copy.62
  15.1 41.3 %all-gather.6.cloned.1.call-done = bf16[4096,512]{0,1:T(8,128)(2,1)} async-done(((bf16[256,512]{0,1:T(8,128)(2,1)}), bf16[4096,512]{0,1:T(8,128)(2,1)}) %all-gather.6.cloned.1.call-update) | async-done | bytes 4194320 | tf_op jit(solution)/shard_map/all_gather | solution.py:124
  56.5 46.8 %all-gather.8.cloned.1.call-done = bf16[4096,512]{0,1:T(8,128)(2,1)} async-done(((bf16[256,512]{0,1:T(8,128)(2,1)}), bf16[4096,512]{0,1:T(8,128)(2,1)}) %all-gather.8.cloned.1.call-update) | async-done | bytes 4194320 | tf_op jit(solution)/shard_map/all_gather | solution.py:125
  103.3 9.0 %while.18 = (s32[]{:T(128)}, f32[4,256]{1,0:T(4,128)S(1)}, f32[4,256]{1,0:T(4,128)S(1)}, f32[4,256,128]{2,1,0:T(8,128)S(1)}, s32[]{:T(128)}, /*index=5*/bf16[409...) while((s32[]{:T(128)}, f32[4,256]{1,0:T(4,128)S(1)}, ...), condition=%wide.region_5.6_spmd.clone, body=%wide.region_0.5_spmd.clone.sunk | while | flops 272633600 | bytes 11085165 | solution.py:74
  104.0 3.1 conditional.3
  104.0 1.3 constant_dynamic-slice_fusion
  105.4 0.2 compare_and_fusion
  105.6 0.6 fusion.22
  106.1 0.3 fusion.3
  106.5 0.7 convolution_add_fusion
  112.3 0.2 copy.63
  112.5 4.8 %convolution_convert_fusion.1 = bf16[256,4096]{1,0:T(8,128)(2,1)} fusion(bf16[256,512]{0,1:T(8,128)(2,1)S(1)} %bitcast.64, bf16[512,4096]{1,0:T(8,128)(2,1)} %param.21), kind=kOutput, calls=%fused_computation.18 | convolution fusion | flops 1074790400 | bytes 6553600 | tf_op jit(solution)/shard_map/dot_general | solution.py:133
  117.4 0.6 copy-done.7
  118.3 59.1 %all-gather.10.cloned.1.call-done = bf16[16,128,1024]{2,1,0:T(8,128)(2,1)} async-done(((bf16[2,128,1024]{2,1,0:T(8,128)(2,1)}), bf16[16,128,1024]{2,1,0:T(8,128)(2,1)}) %all-gather.10.cloned.1.call-update) | async-done | bytes 4194320 | tf_op jit(solution)/shard_map/all_gather | solution.py:161
  177.4 2.9 gather_fusion.1
  180.3 0.4 bitcast_select_fusion.1
  180.7 0.8 copy-done.10
  181.5 1.2 convolution_convert_fusion.3
  182.8 0.5 copy.67
  183.3 3.1 convolution_convert_fusion.2
  186.5 0.5 copy.68
  187.1 1.6 collective-permute-start
  188.6 1.3 collective-permute-done
  189.9 0.3 maximum_maximum_fusion
  190.2 1.3 fusion.23
  191.5 174.4 %all-gather.12.cloned.1.call-done = bf16[2048,4096]{1,0:T(8,128)(2,1)} async-done(((bf16[256,4096]{1,0:T(8,128)(2,1)}), bf16[2048,4096]{1,0:T(8,128)(2,1)}) %all-gather.12.cloned.1.call-update) | async-done | bytes 16777232 | tf_op jit(solution)/shard_map/all_gather | solution.py:15
  365.9 9.2 %reduce_sum.70 = bf16[256,4096]{1,0:T(8,128)(2,1)S(1)} reduce(bf16[8,256,4096]{2,1,0:T(8,128)(2,1)} %bitcast.60, bf16[]{:T(256)} %constant.91.clone.1), dimensions={0}, to_apply=%region_6.7 | reduce | flops 7340032 | bytes 18874370 | tf_op jit(solution)/shard_map/reduce_sum | solution.py:15
  375.1 4.4 convert_add_fusion
  379.5 1.4 fusion.11
  381.1 0.4 fusion.24
  381.5 0.5 fusion.12
  382.0 0.4 copy-done.4
  382.4 0.7 fusion.10
  383.0 0.3 copy.73
  383.4 1.2 copy-done.9
  384.6 2.6 convolution_convert_fusion
  387.2 73.4 %reduce-scatter.2.cloned.1.call-done = bf16[32,4096]{1,0:T(8,128)(2,1)} async-done(((bf16[256,4096]{1,0:T(8,128)(2,1)}), bf16[32,4096]{1,0:T(8,128)(2,1)}) %reduce-scatter.2.cloned.1.call-update) | async-done | bytes 262160 | tf_op jit(solution)/shard_map/reduce_scatter | solution.py:200
  460.6 2.0 convert_add_fusion.1
  (72 shorter events, 1.4 us)
Async XLA Ops:
  6.5 6.0 %copy-start = (bf16[8,128,1024]{2,1,0:T(8,128)(2,1)S(1)}, bf16[8,128,1024]{2,1,0:T(8,128)(2,1)}, u32[]{:S(2)}) copy-start(bf16[8,128,1024]{2,1,0:T(8,128)(2,1)} %param.27) | copy-start | bytes 6291460
  6.5 8.3 %copy-start.5 = (bf16[256,512]{1,0:T(8,128)(2,1)S(1)}, bf16[256,512]{1,0:T(8,128)(2,1)}, u32[]{:S(2)}) copy-start(bf16[256,512]{1,0:T(8,128)(2,1)} %param.18) | copy-start | bytes 786436
  6.5 49.9 %all-gather.6.cloned.1.call-start = ((), (), s32[]{:S(2)}) async-start(), calls=%async_computation.1 | async-start | bytes 4456448 | tf_op jit(solution)/shard_map/all_gather | solution.py:124
  8.6 94.7 %all-gather.8.cloned.1.call-start = ((), (), s32[]{:S(2)}) async-start(), calls=%async_computation.2 | async-start | bytes 4456448 | tf_op jit(solution)/shard_map/all_gather | solution.py:125
  10.4 167.0 %all-gather.10.cloned.1.call-start = ((), (), s32[]{:S(2)}) async-start(), calls=%async_computation.3 | async-start | bytes 4718592 | tf_op jit(solution)/shard_map/all_gather | solution.py:161
  14.1 351.8 %all-gather.12.cloned.1.call-start = ((), (), s32[]{:S(2)}) async-start(), calls=%async_computation.5 | async-start | bytes 18874368 | tf_op jit(solution)/shard_map/all_gather | solution.py:15
  117.3 0.7 copy-start.7
  117.4 343.3 %reduce-scatter.2.cloned.1.call-start = ((), (), s32[]{:S(2)}) async-start(), calls=%async_computation.4 | async-start | bytes 2359296 | tf_op jit(solution)/shard_map/reduce_scatter | solution.py:200
  180.3 1.2 copy-start.10
  181.5 1.3 copy-start.3
  186.5 2.2 copy-start.6
  187.1 2.9 collective-permute-start
  375.1 4.4 copy-start.2
  375.1 4.4 copy-start.8
  381.1 1.3 copy-start.4
  382.4 2.2 copy-start.9
  384.6 78.0 %copy-start.1 = (bf16[8,128,1024]{2,1,0:T(8,128)(2,1)S(1)}, bf16[8,128,1024]{2,1,0:T(8,128)(2,1)}, u32[]{:S(2)}) copy-start(bf16[8,128,1024]{2,1,0:T(8,128)(2,1)} %param.27) | copy-start | bytes 6291460
Sparse Core Ops, SparseCore 0:
  9.0 47.4 all-gather.5
  58.1 45.1 all-gather.7
  105.6 71.7 all-gather.9
  179.6 186.3 all-gather.11
  387.3 73.2 reduce-scatter.1
